TPU v7x, 128 devices: a whole 4x4x4 slice. The times are simulated.
128 devices in a mesh: fsdp: 16 (over z, x_lo, core), rows: 8 (over y, x_hi).
Axes of the slice: x: 4 (x_hi: 2, x_lo: 2; x = x_hi * 2 + x_lo), y: 4, z: 4, core: 2. Of those that a mesh axis runs over, the one named last changes fastest.
Arguments:
- query_rows: bfloat16 [16, 2048, 1536], P('fsdp', 'rows'), may hold values from -6 to 6
- key_rows: bfloat16 [16, 2048, 1536], P('fsdp', 'rows'), may hold values from -6 to 6
- value_rows: bfloat16 [16, 2048, 1536], P('fsdp', 'rows'), may hold values from -6 to 6
- grad_out: bfloat16 [16, 2048, 3072], P('fsdp', 'rows'), may hold values from -6 to 6
- w_out: bfloat16 [1536, 3072], P('fsdp'), may hold values from -0.15625 to 0.15625
Outputs:
- grad_query: bfloat16 [16, 2048, 1536], P('fsdp', 'rows')
- grad_key: bfloat16 [16, 2048, 1536], P('fsdp', 'rows')
- grad_value: bfloat16 [16, 2048, 1536], P('fsdp', 'rows')
- grad_w_out: float32 [1536, 3072], P('fsdp')
All inputs are finite; a program needn't handle non-finite values.
Results may differ from a plain program's by a relative error of at most 0.02.
Values may be sent and summed in bfloat16 or wider, within the bound.
A program may use at most 192 MiB of HBM per device.

v0:
```python
import math
import jax
import jax.numpy as jnp
from jax import lax
from jax.sharding import PartitionSpec as P

HDIM = 128
HEADS = 12
HW = 1536


def in_one_piece(arrays, axis, dim, along):
    both = jnp.concatenate(arrays, axis=along)
    result, at, outs = (lax.all_gather(both, axis, axis=dim, tiled=True), 0, [])
    for a in arrays:
        outs.append(lax.slice_in_dim(result, at, at + a.shape[along], axis=along))
        at += a.shape[along]
    return tuple(outs)


def cut_along(array, dim, devices):
    shape = array.shape
    tiles = array.reshape(*shape[:dim], devices, shape[dim] // devices, *shape[dim + 1 :])
    return jnp.moveaxis(tiles, dim, 0)


def sent_and_summed(array, axis, dim):
    devices = lax.axis_size(axis)
    tiles = lax.all_to_all(cut_along(array, dim, devices), axis, 0, 0, tiled=True)
    return jnp.sum(tiles.astype(jnp.float32), axis=0)


def in_one_piece_2(arrays, axis, dim, along):
    ends, at = ([], 0)
    for a in arrays[:-1]:
        at += a.shape[along]
        ends.append(at)
    both = jnp.concatenate(arrays, axis=along)
    return tuple(jnp.split(sent_and_summed(both, axis, dim), ends, axis=along))


def split_heads(array, count, groups):
    per_group = HEADS // groups
    return jnp.moveaxis(array.reshape(count, groups, per_group, HDIM), 1, 0)


def join_heads(array, count):
    return jnp.moveaxis(array, 0, 1).reshape(count, HW)


def local(query_rows, key_rows, value_rows, grad_out, w_out):
    tokens = query_rows.shape[1]
    factor = 1.0 / math.sqrt(HDIM)
    grad_flat = grad_out[0]
    groups = HEADS // 4
    grad_attn = lax.dot_general(
        grad_flat,
        lax.all_gather(w_out, "fsdp", axis=0, tiled=True),
        (((1,), (1,)), ((), ())),
        preferred_element_type=jnp.float32,
    ).astype(jnp.bfloat16)
    all_keys, all_values = in_one_piece((key_rows, value_rows), "rows", 1, 0)
    length = all_keys.shape[1]

    def attend(inputs):
        query_heads, key_heads, value_heads, grad_heads = inputs
        scores = (
            jnp.einsum("qhd,khd->hqk", query_heads, key_heads, preferred_element_type=jnp.float32)
            * factor
        )
        probs = jax.nn.softmax(scores, axis=-1)
        probs_low = probs.astype(jnp.bfloat16)
        attended = jnp.einsum(
            "hqk,khd->qhd", probs_low, value_heads, preferred_element_type=jnp.float32
        )
        value_part = jnp.einsum(
            "hqk,qhd->khd", probs_low, grad_heads, preferred_element_type=jnp.float32
        )
        grad_probs = jnp.einsum(
            "qhd,khd->hqk", grad_heads, value_heads, preferred_element_type=jnp.float32
        )
        centre = jnp.sum(probs * grad_probs, axis=-1, keepdims=True)
        grad_scores = (probs * (grad_probs - centre)).astype(jnp.bfloat16)
        grad_query = (
            jnp.einsum("hqk,khd->qhd", grad_scores, key_heads, preferred_element_type=jnp.float32)
            * factor
        )
        key_part = (
            jnp.einsum("hqk,qhd->khd", grad_scores, query_heads, preferred_element_type=jnp.float32)
            * factor
        )
        return (
            attended.astype(jnp.bfloat16),
            grad_query.astype(jnp.bfloat16),
            key_part,
            value_part,
        )

    attended, grad_query, key_part, value_part = lax.map(
        attend,
        (
            split_heads(query_rows[0], tokens, groups),
            split_heads(all_keys[0], length, groups),
            split_heads(all_values[0], length, groups),
            split_heads(grad_attn, tokens, groups),
        ),
    )
    attended = join_heads(attended, tokens)
    grad_query = join_heads(grad_query, tokens).reshape(1, tokens, HW)
    key_part = join_heads(key_part, length)
    value_part = join_heads(value_part, length)
    grad_key, grad_value = in_one_piece_2(
        (
            key_part.reshape(1, length, HW).astype(jnp.bfloat16),
            value_part.reshape(1, length, HW).astype(jnp.bfloat16),
        ),
        "rows",
        1,
        0,
    )
    term = lax.dot_general(
        attended, grad_flat, (((0,), (0,)), ((), ())), preferred_element_type=jnp.float32
    )
    partial_grad = sent_and_summed(
        lax.optimization_barrier(term.astype(jnp.bfloat16))
        .astype(jnp.float32)
        .astype(jnp.bfloat16),
        "fsdp",
        0,
    )
    grad_w_out = lax.psum(partial_grad.astype(jnp.bfloat16), "rows").astype(jnp.float32)
    return (grad_query, grad_key.astype(jnp.bfloat16), grad_value.astype(jnp.bfloat16), grad_w_out)


def solution(mesh):
    in_specs = (
        P("fsdp", "rows", None),
        P("fsdp", "rows", None),
        P("fsdp", "rows", None),
        P("fsdp", "rows", None),
        P("fsdp", None),
    )
    out_specs = (
        P("fsdp", "rows", None),
        P("fsdp", "rows", None),
        P("fsdp", "rows", None),
        P("fsdp", None),
    )
    return jax.shard_map(local, mesh=mesh, in_specs=in_specs, out_specs=out_specs, check_vma=False)
```

profile of v0, /device:TPU:0, one launch (start us, length us, event | category | flops | bytes accessed | tf_op | source)
XLA Modules:
  0.0 665.3 jit_solution(4083551851996054782)
XLA Ops:
  13.6 55.7 %all-gather.5.cloned.1.call-done = bf16[1536,3072]{1,0:T(8,128)(2,1)} async-done(((bf16[96,3072]{1,0:T(8,128)(2,1)}), bf16[1536,3072]{1,0:T(8,128)(2,1)}) %all-gather.5.cloned.1.call-update) | async-done | bytes 9437200 | tf_op jit(solution)/shard_map/all_gather | solution.py:58
  69.3 7.2 %convolution_convert_fusion.1 = bf16[256,1536]{1,0:T(8,128)(2,1)} fusion(bf16[1536,3072]{1,0:T(8,128)(2,1)} %all-gather.5.cloned.1.call-done, bf16[1,256,3072]{2,1,0:T(8,128)(2,1)S(1)} %copy-done), kind=kOutput, calls=%fused_computation.48 | convolution fusion | flops 2416312320 | bytes 11796480 | tf_op jit(solution)/shard_map/dot_general | solution.py:56
  79.3 146.3 %all-gather.3.cloned.1.call-done = bf16[2,2048,1536]{1,2,0:T(8,128)(2,1)} async-done(((bf16[2,256,1536]{1,2,0:T(8,128)(2,1)}), bf16[2,2048,1536]{1,2,0:T(8,128)(2,1)}) %all-gather.3.cloned.1.call-update) | async-done | bytes 12582928 | tf_op jit(solution)/shard_map/all_gather | solution.py:14
  225.6 10.6 %fusion.72 = (bf16[1,2048,1536]{1,2,0:T(8,128)(2,1)}, bf16[1,2048,1536]{1,2,0:T(8,128)(2,1)}) fusion(bf16[2,2048,1536]{1,2,0:T(8,128)(2,1)} %all-gather.3.cloned.1.call-done), kind=kLoop, calls=%fused_computation.54 | loop fusion | bytes 25165824 | tf_op jit(solution)/shard_map/slice | solution.py:16
  236.3 125.0 %while.16 = (s32[]{:T(128)}, bf16[3,256,4,128]{1,3,2,0:T(8,128)(2,1)S(1)}, bf16[3,256,4,128]{1,3,2,0:T(8,128)(2,1)}, bf16[3,2048,4,128]{1,3,2,0:T(8,128)(2,1)}, ...) while((s32[]{:T(128)}, ...), condition=%wide.region_4.5_spmd, body=%wide.region_0.4_spmd.sunk | while | flops 3266714624 | bytes 190351520 | solution.py:99
  236.3 2.9 fusion.106
  239.2 4.6 fusion.107
  244.9 9.1 %fusion.108 = bf16[3,256,4,128]{1,3,2,0:T(8,128)(2,1)S(1)} fusion(bf16[3,256,4,128]{1,3,2,0:T(8,128)(2,1)S(1)} %get-tuple-element.193, s32[]{:T(128)S(6)} %copy.79, bf16[3,2048,4,128]{1,3,2,0:T(8,128)(2,1)} %get-tuple-element.207, f32[4,256]{1,0:T(4,128)S(1)} %get-tuple-element.178, f32[4,256,2048]{2,1,0:T(8,128)} %copy-done.1), kind=kOutput, calls=%fused_computation.30.clone.1 | convolution fusion | flops 547490816 | bytes 19141632 | tf_op jit(solution)/shard_map/while/body/eval_jaxpr/hqk,khd->qhd/dot_general | solution.py:73
  254.0 10.0 %bitcast_dynamic-update-slice_fusion.5 = bf16[3,2048,4,128]{1,3,2,0:T(8,128)(2,1)} fusion(bf16[3,2048,4,128]{1,3,2,0:T(8,128)(2,1)} %get-tuple-element.196, s32[]{:T(128)S(6)} %copy.79, bf16[3,256,4,128]{3,1,2,0:T(8,128)(2,1)} %get-tuple-element.210, f32[4,256]{1,0:T(4,128)S(1)} %get-tuple-element.178, f32[4,256,2048]{2,1,0:T(8,128)} %copy-done.1), kind=kOutput, calls=%fused_computation.6.clone.1 | convolution fusion | flops 547359744 | bytes 21238784 | tf_op jit(solution)/shard_map/while/body/eval_jaxpr/hqk,qhd->khd/dot_general | solution.py:76
  264.1 5.6 multiply_reduce_fusion.3
  271.9 3.8 fusion.109
  280.8 4.6 fusion.107
  286.6 9.1 %fusion.108 = bf16[3,256,4,128]{1,3,2,0:T(8,128)(2,1)S(1)} fusion(bf16[3,256,4,128]{1,3,2,0:T(8,128)(2,1)S(1)} %get-tuple-element.193, s32[]{:T(128)S(6)} %copy.79, bf16[3,2048,4,128]{1,3,2,0:T(8,128)(2,1)} %get-tuple-element.207, f32[4,256]{1,0:T(4,128)S(1)} %get-tuple-element.178, f32[4,256,2048]{2,1,0:T(8,128)} %copy-done.1), kind=kOutput, calls=%fused_computation.30.clone.1 | convolution fusion | flops 547490816 | bytes 19141632 | tf_op jit(solution)/shard_map/while/body/eval_jaxpr/hqk,khd->qhd/dot_general | solution.py:73
  295.7 10.1 %bitcast_dynamic-update-slice_fusion.5 = bf16[3,2048,4,128]{1,3,2,0:T(8,128)(2,1)} fusion(bf16[3,2048,4,128]{1,3,2,0:T(8,128)(2,1)} %get-tuple-element.196, s32[]{:T(128)S(6)} %copy.79, bf16[3,256,4,128]{3,1,2,0:T(8,128)(2,1)} %get-tuple-element.210, f32[4,256]{1,0:T(4,128)S(1)} %get-tuple-element.178, f32[4,256,2048]{2,1,0:T(8,128)} %copy-done.1), kind=kOutput, calls=%fused_computation.6.clone.1 | convolution fusion | flops 547359744 | bytes 21238784 | tf_op jit(solution)/shard_map/while/body/eval_jaxpr/hqk,qhd->khd/dot_general | solution.py:76
  305.8 5.6 multiply_reduce_fusion.3
  313.7 3.8 fusion.109
  322.5 4.6 fusion.107
  328.3 9.1 %fusion.108 = bf16[3,256,4,128]{1,3,2,0:T(8,128)(2,1)S(1)} fusion(bf16[3,256,4,128]{1,3,2,0:T(8,128)(2,1)S(1)} %get-tuple-element.193, s32[]{:T(128)S(6)} %copy.79, bf16[3,2048,4,128]{1,3,2,0:T(8,128)(2,1)} %get-tuple-element.207, f32[4,256]{1,0:T(4,128)S(1)} %get-tuple-element.178, f32[4,256,2048]{2,1,0:T(8,128)} %copy-done.1), kind=kOutput, calls=%fused_computation.30.clone.1 | convolution fusion | flops 547490816 | bytes 19141632 | tf_op jit(solution)/shard_map/while/body/eval_jaxpr/hqk,khd->qhd/dot_general | solution.py:73
  337.4 10.0 %bitcast_dynamic-update-slice_fusion.5 = bf16[3,2048,4,128]{1,3,2,0:T(8,128)(2,1)} fusion(bf16[3,2048,4,128]{1,3,2,0:T(8,128)(2,1)} %get-tuple-element.196, s32[]{:T(128)S(6)} %copy.79, bf16[3,256,4,128]{3,1,2,0:T(8,128)(2,1)} %get-tuple-element.210, f32[4,256]{1,0:T(4,128)S(1)} %get-tuple-element.178, f32[4,256,2048]{2,1,0:T(8,128)} %copy-done.1), kind=kOutput, calls=%fused_computation.6.clone.1 | convolution fusion | flops 547359744 | bytes 21238784 | tf_op jit(solution)/shard_map/while/body/eval_jaxpr/hqk,qhd->khd/dot_general | solution.py:76
  347.4 5.6 multiply_reduce_fusion.3
  355.2 3.8 fusion.109
  361.2 5.1 convolution_convert_fusion
  366.3 4.8 all-to-all-start.1
  371.1 5.5 copy.67
  376.6 5.5 copy.66
  383.4 7.8 %copy.52 = bf16[8,2,256,1536]{2,3,1,0:T(8,128)(2,1)} copy(bf16[8,2,256,1536]{2,0,3,1:T(8,128)(2,1)S(1)} %maximum_bitcast_fusion) | data formatting | bytes 25165824 | tf_op jit(solution)/shard_map/transpose | solution.py:24
  391.2 86.4 %all-to-all-done.1 = bf16[16,96,3072]{2,1,0:T(8,128)(2,1)} async-done(((bf16[16,96,3072]{2,1,0:T(8,128)(2,1)}), bf16[16,96,3072]{2,1,0:T(8,128)(2,1)}, u32[]{:S(2)}, u32[]{:S(2)}) %all-to-all-start.1) | async-done | bytes 9437216 | tf_op jit(solution)/shard_map/all_to_all | solution.py:29
  477.7 5.4 all-to-all-start
  483.4 6.5 reduce_sum.40
  491.1 93.4 %all-reduce.2.cloned.1.call-done = bf16[96,3072]{1,0:T(8,128)(2,1)} async-done(((bf16[96,3072]{1,0:T(8,128)(2,1)}), bf16[96,3072]{1,0:T(8,128)(2,1)}) %all-reduce.2.cloned.1.call-update) | async-done | bytes 589840 | tf_op jit(solution)/shard_map/psum | solution.py:131
  586.7 59.4 %all-to-all-done = bf16[8,2,256,1536]{2,3,1,0:T(8,128)(2,1)} async-done(((bf16[8,2,256,1536]{2,3,1,0:T(8,128)(2,1)}), bf16[8,2,256,1536]{2,3,1,0:T(8,128)(2,1)}, u32[]{:S(2)}, u32[]{:S(2)}) %all-to-all-start) | async-done | bytes 12582944 | tf_op jit(solution)/shard_map/all_to_all | solution.py:29
  646.1 6.8 %reduce.1 = bf16[2,256,1536]{1,2,0:T(8,128)(2,1)S(1)} reduce(bf16[8,2,256,1536]{2,3,1,0:T(8,128)(2,1)} %all-to-all-done, bf16[]{:T(256)} %constant.32.clone.1), dimensions={0}, to_apply=%region_5.6.clone | reduce | flops 5505024 | bytes 14155778 | tf_op jit(solution)/shard_map/reduce_sum | solution.py:30
  (48 shorter events, 42.3 us)
Async XLA Ops:
  7.2 62.2 %copy-start = (bf16[1,256,3072]{2,1,0:T(8,128)(2,1)S(1)}, bf16[1,256,3072]{2,1,0:T(8,128)(2,1)}, u32[]{:S(2)}) copy-start(bf16[1,256,3072]{2,1,0:T(8,128)(2,1)} %param.10) | copy-start | bytes 4718596
  7.2 62.1 %all-gather.5.cloned.1.call-start = ((), (), s32[]{:S(2)}) async-start(), calls=%async_computation.3 | async-start | bytes 10027008 | tf_op jit(solution)/shard_map/all_gather | solution.py:58
  7.9 217.7 %all-gather.3.cloned.1.call-start = ((), (), s32[]{:S(2)}) async-start(), calls=%async_computation.2 | async-start | bytes 14155776 | tf_op jit(solution)/shard_map/all_gather | solution.py:14
  79.3 157.0 %copy-start.3 = (bf16[3,256,4,128]{1,3,2,0:T(8,128)(2,1)S(1)}, bf16[3,256,4,128]{1,3,2,0:T(8,128)(2,1)}, u32[]{:S(2)}) copy-start(bf16[3,256,4,128]{1,3,2,0:T(8,128)(2,1)} %custom-call) | copy-start | bytes 2359300
  239.1 5.8 copy-start.1
  264.1 6.5 copy-start.2
  280.8 5.8 copy-start.1
  305.8 6.5 copy-start.2
  322.5 5.8 copy-start.1
  347.4 6.5 copy-start.2
  366.3 111.4 %all-to-all-start.1 = ((bf16[16,96,3072]{2,1,0:T(8,128)(2,1)}), bf16[16,96,3072]{2,1,0:T(8,128)(2,1)}, u32[]{:S(2)}, u32[]{:S(2)}) async-start(bf16[16,96,3072]{2,1,0:T(8,128)(2,1)} %bitcast.137), calls=%async_computation.1 | async-start | bytes 18874368 | tf_op jit(solution)/shard_map/all_to_all | solution.py:29
  477.7 168.4 %all-to-all-start = ((bf16[8,2,256,1536]{2,3,1,0:T(8,128)(2,1)}), bf16[8,2,256,1536]{2,3,1,0:T(8,128)(2,1)}, u32[]{:S(2)}, u32[]{:S(2)}) async-start(bf16[8,2,256,1536]{2,3,1,0:T(8,128)(2,1)} %copy.52), calls=%async_computation | async-start | bytes 25165824 | tf_op jit(solution)/shard_map/all_to_all | solution.py:29
  483.1 6.9 %copy-start.4 = (bf16[3,256,4,128]{1,3,2,0:T(8,128)(2,1)S(1)}, bf16[3,256,4,128]{1,3,2,0:T(8,128)(2,1)}, u32[]{:S(2)}) copy-start(bf16[3,256,4,128]{1,3,2,0:T(8,128)(2,1)} %get-tuple-element.54) | copy-start | bytes 2359300
  483.1 101.4 %all-reduce.2.cloned.1.call-start = ((), (), s32[]{:S(2)}) async-start(), calls=%async_computation.4 | async-start | bytes 1179648 | tf_op jit(solution)/shard_map/psum | solution.py:131
Sparse Core Ops, SparseCore 0:
  9.7 59.5 all-gather.4
  71.5 154.0 all-gather.2
  490.1 94.3 all-reduce.1
where the time goes:
time: 666 us; the launch traced here: 665 us
  waiting for transfers between devices  442 us (66%)
  matrix products  113 us (17%)
  local copies, waits for them, and re-layouts  49.6 us (7%)
  other arithmetic  36.1 us (5%)
  between operations  13.9 us (2%)
  starting transfers between devices  10.6 us (2%)
    all_gather x1, waiting for transfers between devices, in_one_piece(): result, at, outs = (lax.all_gather(both, axis, axis=dim, tiled=True), 0, [])  146 us
    all_to_all x2, waiting for transfers between devices, sent_and_summed(): lax.all_to_all(cut_along(array, dim, devices), axis, 0, 0, tiled=True)  146 us
    psum x1, waiting for transfers between devices, local(): lax.psum(partial_grad.astype(jnp.bfloat16), 'rows').astype(jnp.float32)  93.4 us
    all_gather x1, waiting for transfers between devices, local(): lax.all_gather(w_out, 'fsdp', axis=0, tiled=True)  55.7 us
    dot_general x3, matrix products, attend(): jnp.einsum('hqk,qhd->khd', probs_low, grad_heads, preferred_element_type=...  30.1 us
    dot_general x3, matrix products, attend(): jnp.einsum('hqk,khd->qhd', probs_low, value_heads, preferred_element_type...  27.3 us
    unnamed x13, local copies, waits for them, and re-layouts  19.9 us
    dot_general x3, matrix products, attend(): jnp.einsum('qhd,khd->hqk', grad_heads, value_heads, preferred_element_typ...  16.8 us
  transfers between devices with their start and end apart: 5, of which 5 were waited for; matrix products, arithmetic and copies ran while one was open for 7% of the time, Pallas kernels for 0%

commit v1 on v0

--- a/solution.py
+++ b/solution.py
@@ -7,6 +7,18 @@
 HDIM = 128
 HEADS = 12
 HW = 1536
+
+
+def fix_digits_by_axis(payload, mesh_name):
+    return jnp.concatenate(
+        lax.all_to_all(
+            jnp.stack([payload for _ in range(lax.axis_size(mesh_name))], axis=0),
+            split_axis=0,
+            concat_axis=0,
+            axis_name=mesh_name,
+        ),
+        axis=0,
+    )
 
 
 def in_one_piece(arrays, axis, dim, along):
@@ -55,7 +67,7 @@
     groups = HEADS // 4
     grad_attn = lax.dot_general(
         grad_flat,
-        lax.all_gather(w_out, "fsdp", axis=0, tiled=True),
+        fix_digits_by_axis(w_out, "fsdp"),
         (((1,), (1,)), ((), ())),
         preferred_element_type=jnp.float32,
     ).astype(jnp.bfloat16)

time: 666 us -> 677 us (1.017)
    all_to_all x0 -> x1, waiting for transfers between devices: none -> 174 us  [fix_digits_by_axis(): lax.all_to_all(jnp.stack([payload for _ in range(lax.axis_size(mesh_name)...]
    all_gather x1, waiting for transfers between devices: 146 us -> 27.6 us  [in_one_piece(): result, at, outs = (lax.all_gather(both, axis, axis=dim, tiled=True), 0, [])]
    all_gather x1 -> x0, waiting for transfers between devices: 55.7 us -> none  [local(): lax.all_gather(w_out, 'fsdp', axis=0, tiled=True)]
    unnamed x13 -> x15, local copies, waits for them, and re-layouts: 19.9 us -> 18.8 us
where the time goes in v1:
time: 677 us; the launch traced here: 676 us
  waiting for transfers between devices  441 us (65%)
  matrix products  113 us (17%)
  local copies, waits for them, and re-layouts  54.2 us (8%)
  other arithmetic  36.1 us (5%)
  starting transfers between devices  17.2 us (3%)
  between operations  14.2 us (2%)
    all_to_all x1, waiting for transfers between devices, fix_digits_by_axis(): lax.all_to_all(jnp.stack([payload for _ in range(lax.axis_size(mesh_name)...  174 us
    all_to_all x2, waiting for transfers between devices, sent_and_summed(): lax.all_to_all(cut_along(array, dim, devices), axis, 0, 0, tiled=True)  146 us
    psum x1, waiting for transfers between devices, local(): lax.psum(partial_grad.astype(jnp.bfloat16), 'rows').astype(jnp.float32)  93.4 us
    dot_general x3, matrix products, attend(): jnp.einsum('hqk,qhd->khd', probs_low, grad_heads, preferred_element_type=...  30.1 us
    all_gather x1, waiting for transfers between devices, in_one_piece(): result, at, outs = (lax.all_gather(both, axis, axis=dim, tiled=True), 0, [])  27.6 us
    dot_general x3, matrix products, attend(): jnp.einsum('hqk,khd->qhd', probs_low, value_heads, preferred_element_type...  27.3 us
    unnamed x15, local copies, waits for them, and re-layouts  18.8 us
    dot_general x3, matrix products, attend(): jnp.einsum('qhd,khd->hqk', grad_heads, value_heads, preferred_element_typ...  16.8 us
  transfers between devices with their start and end apart: 5, of which 5 were waited for; matrix products, arithmetic and copies ran while one was open for 7% of the time, Pallas kernels for 0%

profile of v1, /device:TPU:0, one launch (start us, length us, event | category | flops | bytes accessed | tf_op | source)
XLA Modules:
  0.0 676.0 jit_solution(1857903228667347604)
XLA Ops:
  11.5 5.9 stack.2
  17.4 6.6 all-to-all-start
  24.3 174.3 %all-to-all-done = bf16[16,96,3072]{2,1,0:T(8,128)(2,1)} async-done(((bf16[16,96,3072]{2,1,0:T(8,128)(2,1)}), bf16[16,96,3072]{2,1,0:T(8,128)(2,1)}, u32[]{:S(2)}, u32[]{:S(2)}) %all-to-all-start) | async-done | bytes 9437216 | tf_op jit(solution)/shard_map/all_to_all | solution.py:14
  198.6 7.2 %convolution_convert_fusion.1 = bf16[256,1536]{1,0:T(8,128)(2,1)} fusion(bf16[1536,3072]{1,0:T(8,128)(2,1)} %bitcast.19, bf16[1,256,3072]{2,1,0:T(8,128)(2,1)S(1)} %copy-done), kind=kOutput, calls=%fused_computation.48 | convolution fusion | flops 2416312320 | bytes 11796480 | tf_op jit(solution)/shard_map/dot_general | solution.py:68
  208.6 27.6 %all-gather.2.cloned.1.call-done = bf16[2,2048,1536]{1,2,0:T(8,128)(2,1)} async-done(((bf16[2,256,1536]{1,2,0:T(8,128)(2,1)}), bf16[2,2048,1536]{1,2,0:T(8,128)(2,1)}) %all-gather.2.cloned.1.call-update) | async-done | bytes 12582928 | tf_op jit(solution)/shard_map/all_gather | solution.py:26
  236.2 10.6 %fusion.72 = (bf16[1,2048,1536]{1,2,0:T(8,128)(2,1)}, bf16[1,2048,1536]{1,2,0:T(8,128)(2,1)}) fusion(bf16[2,2048,1536]{1,2,0:T(8,128)(2,1)} %all-gather.2.cloned.1.call-done), kind=kLoop, calls=%fused_computation.54 | loop fusion | bytes 25165824 | tf_op jit(solution)/shard_map/slice | solution.py:28
  246.8 124.8 %while.16 = (s32[]{:T(128)}, bf16[3,256,4,128]{1,3,2,0:T(8,128)(2,1)S(1)}, bf16[3,256,4,128]{1,3,2,0:T(8,128)(2,1)}, bf16[3,2048,4,128]{1,3,2,0:T(8,128)(2,1)}, ...) while((s32[]{:T(128)}, ...), condition=%wide.region_4.5_spmd, body=%wide.region_0.4_spmd.sunk | while | flops 3266714624 | bytes 190351520 | solution.py:111
  249.7 4.6 fusion.107
  255.4 9.1 %fusion.108 = bf16[3,256,4,128]{1,3,2,0:T(8,128)(2,1)S(1)} fusion(bf16[3,256,4,128]{1,3,2,0:T(8,128)(2,1)S(1)} %get-tuple-element.193, s32[]{:T(128)S(6)} %copy.79, bf16[3,2048,4,128]{1,3,2,0:T(8,128)(2,1)} %get-tuple-element.207, f32[4,256]{1,0:T(4,128)S(1)} %get-tuple-element.178, f32[4,256,2048]{2,1,0:T(8,128)} %copy-done.1), kind=kOutput, calls=%fused_computation.30.clone.1 | convolution fusion | flops 547490816 | bytes 19141632 | tf_op jit(solution)/shard_map/while/body/eval_jaxpr/hqk,khd->qhd/dot_general | solution.py:85
  264.5 10.0 %bitcast_dynamic-update-slice_fusion.5 = bf16[3,2048,4,128]{1,3,2,0:T(8,128)(2,1)} fusion(bf16[3,2048,4,128]{1,3,2,0:T(8,128)(2,1)} %get-tuple-element.196, s32[]{:T(128)S(6)} %copy.79, bf16[3,256,4,128]{3,1,2,0:T(8,128)(2,1)} %get-tuple-element.210, f32[4,256]{1,0:T(4,128)S(1)} %get-tuple-element.178, f32[4,256,2048]{2,1,0:T(8,128)} %copy-done.1), kind=kOutput, calls=%fused_computation.6.clone.1 | convolution fusion | flops 547359744 | bytes 21238784 | tf_op jit(solution)/shard_map/while/body/eval_jaxpr/hqk,qhd->khd/dot_general | solution.py:88
  274.6 5.6 multiply_reduce_fusion.3
  282.4 3.8 fusion.109
  291.3 4.6 fusion.107
  297.0 9.1 %fusion.108 = bf16[3,256,4,128]{1,3,2,0:T(8,128)(2,1)S(1)} fusion(bf16[3,256,4,128]{1,3,2,0:T(8,128)(2,1)S(1)} %get-tuple-element.193, s32[]{:T(128)S(6)} %copy.79, bf16[3,2048,4,128]{1,3,2,0:T(8,128)(2,1)} %get-tuple-element.207, f32[4,256]{1,0:T(4,128)S(1)} %get-tuple-element.178, f32[4,256,2048]{2,1,0:T(8,128)} %copy-done.1), kind=kOutput, calls=%fused_computation.30.clone.1 | convolution fusion | flops 547490816 | bytes 19141632 | tf_op jit(solution)/shard_map/while/body/eval_jaxpr/hqk,khd->qhd/dot_general | solution.py:85
  306.1 10.0 %bitcast_dynamic-update-slice_fusion.5 = bf16[3,2048,4,128]{1,3,2,0:T(8,128)(2,1)} fusion(bf16[3,2048,4,128]{1,3,2,0:T(8,128)(2,1)} %get-tuple-element.196, s32[]{:T(128)S(6)} %copy.79, bf16[3,256,4,128]{3,1,2,0:T(8,128)(2,1)} %get-tuple-element.210, f32[4,256]{1,0:T(4,128)S(1)} %get-tuple-element.178, f32[4,256,2048]{2,1,0:T(8,128)} %copy-done.1), kind=kOutput, calls=%fused_computation.6.clone.1 | convolution fusion | flops 547359744 | bytes 21238784 | tf_op jit(solution)/shard_map/while/body/eval_jaxpr/hqk,qhd->khd/dot_general | solution.py:88
  316.1 5.6 multiply_reduce_fusion.3
  324.0 3.8 fusion.109
  332.9 4.6 fusion.107
  338.6 9.1 %fusion.108 = bf16[3,256,4,128]{1,3,2,0:T(8,128)(2,1)S(1)} fusion(bf16[3,256,4,128]{1,3,2,0:T(8,128)(2,1)S(1)} %get-tuple-element.193, s32[]{:T(128)S(6)} %copy.79, bf16[3,2048,4,128]{1,3,2,0:T(8,128)(2,1)} %get-tuple-element.207, f32[4,256]{1,0:T(4,128)S(1)} %get-tuple-element.178, f32[4,256,2048]{2,1,0:T(8,128)} %copy-done.1), kind=kOutput, calls=%fused_computation.30.clone.1 | convolution fusion | flops 547490816 | bytes 19141632 | tf_op jit(solution)/shard_map/while/body/eval_jaxpr/hqk,khd->qhd/dot_general | solution.py:85
  347.7 10.1 %bitcast_dynamic-update-slice_fusion.5 = bf16[3,2048,4,128]{1,3,2,0:T(8,128)(2,1)} fusion(bf16[3,2048,4,128]{1,3,2,0:T(8,128)(2,1)} %get-tuple-element.196, s32[]{:T(128)S(6)} %copy.79, bf16[3,256,4,128]{3,1,2,0:T(8,128)(2,1)} %get-tuple-element.210, f32[4,256]{1,0:T(4,128)S(1)} %get-tuple-element.178, f32[4,256,2048]{2,1,0:T(8,128)} %copy-done.1), kind=kOutput, calls=%fused_computation.6.clone.1 | convolution fusion | flops 547359744 | bytes 21238784 | tf_op jit(solution)/shard_map/while/body/eval_jaxpr/hqk,qhd->khd/dot_general | solution.py:88
  357.8 5.6 multiply_reduce_fusion.3
  371.6 5.1 convolution_convert_fusion
  376.7 4.8 all-to-all-start.2
  381.6 5.5 copy.67
  387.1 5.5 copy.66
  393.9 7.8 %copy.52 = bf16[8,2,256,1536]{2,3,1,0:T(8,128)(2,1)} copy(bf16[8,2,256,1536]{2,0,3,1:T(8,128)(2,1)S(1)} %maximum_bitcast_fusion) | data formatting | bytes 25165824 | tf_op jit(solution)/shard_map/transpose | solution.py:36
  401.7 86.4 %all-to-all-done.2 = bf16[16,96,3072]{2,1,0:T(8,128)(2,1)} async-done(((bf16[16,96,3072]{2,1,0:T(8,128)(2,1)}), bf16[16,96,3072]{2,1,0:T(8,128)(2,1)}, u32[]{:S(2)}, u32[]{:S(2)}) %all-to-all-start.2) | async-done | bytes 9437216 | tf_op jit(solution)/shard_map/all_to_all | solution.py:41
  488.1 5.4 all-to-all-start.1
  493.8 6.5 reduce_sum.40
  501.6 93.4 %all-reduce.2.cloned.1.call-done = bf16[96,3072]{1,0:T(8,128)(2,1)} async-done(((bf16[96,3072]{1,0:T(8,128)(2,1)}), bf16[96,3072]{1,0:T(8,128)(2,1)}) %all-reduce.2.cloned.1.call-update) | async-done | bytes 589840 | tf_op jit(solution)/shard_map/psum | solution.py:143
  597.1 59.4 %all-to-all-done.1 = bf16[8,2,256,1536]{2,3,1,0:T(8,128)(2,1)} async-done(((bf16[8,2,256,1536]{2,3,1,0:T(8,128)(2,1)}), bf16[8,2,256,1536]{2,3,1,0:T(8,128)(2,1)}, u32[]{:S(2)}, u32[]{:S(2)}) %all-to-all-start.1) | async-done | bytes 12582944 | tf_op jit(solution)/shard_map/all_to_all | solution.py:41
  656.5 6.8 %reduce.1 = bf16[2,256,1536]{1,2,0:T(8,128)(2,1)S(1)} reduce(bf16[8,2,256,1536]{2,3,1,0:T(8,128)(2,1)} %all-to-all-done.1, bf16[]{:T(256)} %constant.32.clone.1), dimensions={0}, to_apply=%region_5.6.clone | reduce | flops 5505024 | bytes 14155778 | tf_op jit(solution)/shard_map/reduce_sum | solution.py:42
  (50 shorter events, 47.1 us)
Async XLA Ops:
  7.2 191.5 %copy-start = (bf16[1,256,3072]{2,1,0:T(8,128)(2,1)S(1)}, bf16[1,256,3072]{2,1,0:T(8,128)(2,1)}, u32[]{:S(2)}) copy-start(bf16[1,256,3072]{2,1,0:T(8,128)(2,1)} %param.10) | copy-start | bytes 4718596
  7.2 229.0 %all-gather.2.cloned.1.call-start = ((), (), s32[]{:S(2)}) async-start(), calls=%async_computation.3 | async-start | bytes 14155776 | tf_op jit(solution)/shard_map/all_gather | solution.py:26
  17.4 6.7 copy-start.4
  17.4 181.2 %all-to-all-start = ((bf16[16,96,3072]{2,1,0:T(8,128)(2,1)}), bf16[16,96,3072]{2,1,0:T(8,128)(2,1)}, u32[]{:S(2)}, u32[]{:S(2)}) async-start(bf16[16,96,3072]{2,1,0:T(8,128)(2,1)} %stack.2), calls=%async_computation | async-start | bytes 18874368 | tf_op jit(solution)/shard_map/all_to_all | solution.py:14
  208.6 38.2 %copy-start.3 = (bf16[3,256,4,128]{1,3,2,0:T(8,128)(2,1)S(1)}, bf16[3,256,4,128]{1,3,2,0:T(8,128)(2,1)}, u32[]{:S(2)}) copy-start(bf16[3,256,4,128]{1,3,2,0:T(8,128)(2,1)} %custom-call) | copy-start | bytes 2359300
  249.7 5.7 copy-start.1
  274.6 6.5 copy-start.2
  291.3 5.7 copy-start.1
  316.1 6.5 copy-start.2
  332.9 5.7 copy-start.1
  357.8 6.5 copy-start.2
  376.7 111.4 %all-to-all-start.2 = ((bf16[16,96,3072]{2,1,0:T(8,128)(2,1)}), bf16[16,96,3072]{2,1,0:T(8,128)(2,1)}, u32[]{:S(2)}, u32[]{:S(2)}) async-start(bf16[16,96,3072]{2,1,0:T(8,128)(2,1)} %bitcast.138), calls=%async_computation.2 | async-start | bytes 18874368 | tf_op jit(solution)/shard_map/all_to_all | solution.py:41
  488.1 168.4 %all-to-all-start.1 = ((bf16[8,2,256,1536]{2,3,1,0:T(8,128)(2,1)}), bf16[8,2,256,1536]{2,3,1,0:T(8,128)(2,1)}, u32[]{:S(2)}, u32[]{:S(2)}) async-start(bf16[8,2,256,1536]{2,3,1,0:T(8,128)(2,1)} %copy.52), calls=%async_computation.1 | async-start | bytes 25165824 | tf_op jit(solution)/shard_map/all_to_all | solution.py:41
  493.5 6.9 %copy-start.5 = (bf16[3,256,4,128]{1,3,2,0:T(8,128)(2,1)S(1)}, bf16[3,256,4,128]{1,3,2,0:T(8,128)(2,1)}, u32[]{:S(2)}) copy-start(bf16[3,256,4,128]{1,3,2,0:T(8,128)(2,1)} %get-tuple-element.54) | copy-start | bytes 2359300
  493.5 101.4 %all-reduce.2.cloned.1.call-start = ((), (), s32[]{:S(2)}) async-start(), calls=%async_computation.4 | async-start | bytes 1179648 | tf_op jit(solution)/shard_map/psum | solution.py:143
Sparse Core Ops, SparseCore 0:
  11.6 224.5 all-gather.1
  500.5 94.3 all-reduce.1
